TPU v7x, 32 devices: a whole 2x2x4 slice. The times are simulated.
32 devices in a mesh: dp: 8 (over z, x), seq: 4 (over y, core).
Axes of the slice: x: 2, y: 2, z: 4, core: 2. Of those that a mesh axis runs over, the one named last changes fastest.
Arguments:
- field: bfloat16 [8, 2048, 1024], P('dp', 'seq'), may hold values from -6 to 6
- eq_embed: bfloat16 [8, 512, 1024], P('dp', 'seq'), may hold values from -6 to 6
- eq_len: int32 [8], replicated, may hold values from 1 to 512, 2048 in all
- owner: int32 [8], replicated, may hold values from 0 to 7, as said below
- norm_gain: float32 [1024], replicated, may hold values from 0.1 to 1.9
- w_qkv: bfloat16 [1024, 3072], replicated, may hold values from -0.176776695 to 0.176776695
- w_out: bfloat16 [1024, 1024], replicated, may hold values from -0.1875 to 0.1875
- cross_gain: float32 [1024], replicated, may hold values from 0.1 to 1.9
- w_cq: bfloat16 [1024, 1024], replicated, may hold values from -0.125 to 0.125
- w_ckv: bfloat16 [1024, 2048], replicated, may hold values from -0.125 to 0.125
- w_cout: bfloat16 [1024, 1024], replicated, may hold values from -0.1875 to 0.1875
Outputs:
- joined: bfloat16 [8, 2048, 1024], P('dp', 'seq')
Inputs may be any that keep to these rules, and one draw needn't show every extreme that they name: `owner`: every slot number appears exactly once. `eq_len`: some slot has all 512 tokens real.
All inputs are finite; a program needn't handle non-finite values.
Results may differ from a plain program's by a relative error of at most 0.0055.
Values may be sent and summed in bfloat16 or wider, within the bound.
A program may use at most 128 MiB of HBM per device.

v0:
```python
import jax
import jax.numpy as jnp
from jax import lax
from jax.sharding import PartitionSpec as P

D = 1024
HEADS = 16
HEAD_DIM = 64


def normalize(values, gain):
    return values * lax.rsqrt(jnp.mean(values * values, axis=-1, keepdims=True) + 1e-06) * gain


def attend(query, keys, values, valid):
    rows = query.shape[0]
    heads = query.shape[1]
    depth = query.shape[2]
    block = min(512, rows)
    scale = depth ** (-0.5)

    def one_block(query_block):
        scores = (
            jnp.einsum("qhd,khd->hqk", query_block, keys, preferred_element_type=jnp.float32)
            * scale
        )
        expo = jnp.where(valid[None, None, :], jnp.exp(scores), 0.0)
        weights = (expo / jnp.sum(expo, axis=-1, keepdims=True)).astype(jnp.bfloat16)
        return jnp.einsum(
            "hqk,khd->qhd", weights, values, preferred_element_type=jnp.float32
        ).astype(jnp.bfloat16)

    blocks = lax.map(one_block, query.reshape(rows // block, block, heads, depth))
    return blocks.reshape(rows, heads * depth)


def pick_slot(wanted, carry, piece):
    inside = (wanted >= 0) & (wanted < piece.shape[0])
    picked = lax.dynamic_index_in_dim(
        piece, jnp.clip(wanted, 0, piece.shape[0] - 1), 0, keepdims=False
    )
    return jnp.where(inside, picked, carry)


def per_device(
    field, eq_embed, eq_len, owner, norm_gain, w_qkv, w_out, cross_gain, w_cq, w_ckv, w_cout
):
    tokens = field[0].astype(jnp.float32)
    tok_rows = tokens.shape[0]
    groups = lax.axis_size("seq")
    head_count = HEADS // groups
    normed = normalize(tokens, norm_gain).astype(jnp.bfloat16)
    projected = jnp.dot(normed, w_qkv, preferred_element_type=jnp.float32).astype(jnp.bfloat16)
    stacked = projected.reshape(tok_rows, 3, D)
    local_heads = lax.all_to_all(stacked, "seq", split_axis=2, concat_axis=0, tiled=True)
    seq_rows = local_heads.shape[0]
    split = local_heads.reshape(seq_rows, 3, head_count, HEAD_DIM)
    every = jnp.ones((seq_rows,), dtype=bool)
    attended = attend(split[:, 0], split[:, 1], split[:, 2], every)
    merged = lax.all_to_all(attended, "seq", split_axis=0, concat_axis=1, tiled=True)
    mixed = tokens + jnp.dot(merged, w_out, preferred_element_type=jnp.float32)
    cross_in = normalize(mixed, cross_gain).astype(jnp.bfloat16)
    cross_q = jnp.dot(cross_in, w_cq, preferred_element_type=jnp.float32).astype(jnp.bfloat16)
    slot = lax.dynamic_index_in_dim(owner, lax.axis_index("dp"), 0, keepdims=False)
    length = lax.dynamic_index_in_dim(eq_len, slot, 0, keepdims=False)
    eq_rows = eq_embed.shape[1]
    empty = jnp.zeros(eq_embed.shape[1:], jnp.bfloat16)
    owned_rows = pick_slot(slot, empty, lax.all_gather(eq_embed, "dp", axis=0, tiled=True))
    owned_kv = jnp.dot(owned_rows, w_ckv, preferred_element_type=jnp.float32).astype(jnp.bfloat16)
    whole_kv = lax.all_gather(owned_kv, "seq", axis=0, tiled=True)
    whole_kv = whole_kv.reshape(eq_rows * groups, 2, HEADS, HEAD_DIM)
    valid = jnp.arange(eq_rows * groups, dtype=jnp.int32) < length
    cross_att = attend(
        cross_q.reshape(tok_rows, HEADS, HEAD_DIM), whole_kv[:, 0], whole_kv[:, 1], valid
    )
    joined = mixed + jnp.dot(cross_att, w_cout, preferred_element_type=jnp.float32)
    return joined.astype(jnp.bfloat16)[None]


def solution(mesh):
    in_specs = (
        P("dp", "seq", None),
        P("dp", "seq", None),
        P(),
        P(),
        P(),
        P(),
        P(),
        P(),
        P(),
        P(),
        P(),
    )
    out_specs = P("dp", "seq", None)
    return jax.shard_map(
        per_device, mesh=mesh, in_specs=in_specs, out_specs=out_specs, check_vma=False
    )
```

profile of v0, /device:TPU:0, one launch (start us, length us, event | category | flops | bytes accessed | tf_op | source)
XLA Modules:
  0.0 189.4 jit_solution(14081409868850262506)
XLA Ops:
  6.5 0.0 copy-start
  6.5 0.0 all-gather.3.cloned.1.call-start
  6.5 0.7 all-gather.3.cloned.1.call-update
  7.3 1.5 fusion.12
  8.8 8.3 %convolution_convert_fusion = bf16[512,3072]{1,0:T(8,128)(2,1)} fusion(bf16[1024,3072]{1,0:T(8,128)(2,1)} %param.18, bf16[1,512,1024]{2,1,0:T(8,128)(2,1)} %param.13, f32[1024]{0:T(1024)} %param.17, f32[512]{0:T(512)S(1)} %add_rsqrt_fusion.1), kind=kOutput, calls=%fused_computation.16 | convolution fusion | flops 3224895488 | bytes 10491904 | tf_op jit(solution)/shard_map/dot_general | solution.py:53
  17.1 4.7 %copy.28 = bf16[512,3072]{0,1:T(8,128)(2,1)} copy(bf16[512,3072]{1,0:T(8,128)(2,1)} %convolution_convert_fusion) | data formatting | bytes 6291456 | tf_op jit(solution)/shard_map/convert_element_type | solution.py:53
  21.7 6.5 %copy.29 = bf16[512,3,1024]{0,1,2:T(4,128)(2,1)} copy(bf16[512,3,1024]{0,2,1:T(8,128)(2,1)} %bitcast.75) | data formatting | bytes 6291456 | tf_op jit(solution)/shard_map/reshape | solution.py:54
  28.3 5.0 %all-to-all-start = ((bf16[512,3,1024]{0,1,2:T(4,128)(2,1)}), bf16[512,3,1024]{0,1,2:T(4,128)(2,1)}, u32[]{:S(2)}, u32[]{:S(2)}) async-start(bf16[512,3,1024]{0,1,2:T(4,128)(2,1)} %copy.29), calls=%async_computation | async-start | bytes 8388608 | tf_op jit(solution)/shard_map/all_to_all | solution.py:55
  33.3 0.2 all-gather.5.cloned.1.call-start
  33.5 0.0 copy-done.8
  33.5 0.6 dynamic_slice.18
  35.8 46.4 %all-to-all-done = bf16[512,3,1024]{0,1,2:T(4,128)(2,1)} async-done(((bf16[512,3,1024]{0,1,2:T(4,128)(2,1)}), bf16[512,3,1024]{0,1,2:T(4,128)(2,1)}, u32[]{:S(2)}, u32[]{:S(2)}) %all-to-all-start) | async-done | bytes 3145760 | tf_op jit(solution)/shard_map/all_to_all | solution.py:55
  82.2 3.0 %copy.30 = bf16[512,3,1024]{0,2,1:T(8,128)(2,1)S(1)} copy(bf16[512,3,1024]{0,1,2:T(4,128)(2,1)} %all-to-all-done) | data formatting | bytes 6291456 | tf_op jit(solution)/shard_map/all_to_all | solution.py:55
  85.1 4.1 %copy.31 = bf16[4,512,3,256]{1,0,3,2:T(4,128)(2,1)} copy(bf16[4,512,3,256]{1,3,0,2:T(8,128)(2,1)S(1)} %bitcast.76) | data formatting | bytes 6291456 | tf_op jit(solution)/shard_map/all_to_all | solution.py:55
  89.2 6.1 %reshape.50 = bf16[2048,3,4,64]{0,3,2,1:T(8,128)(2,1)} reshape(bf16[4,512,3,256]{1,0,3,2:T(4,128)(2,1)} %copy.31) | data formatting | bytes 6291456 | tf_op jit(solution)/shard_map/reshape | solution.py:57
  95.3 3.6 %slice_bitcast_fusion.4 = (bf16[2048,4,64]{0,2,1:T(8,128)(2,1)}, bf16[2048,4,64]{0,2,1:T(8,128)(2,1)S(1)}, bf16[2048,1,4,64]{0,3,2,1:T(8,128)(2,1)}) fusion(bf16[2048,3,4,64]{0,3,2,1:T(8,128)(2,1)} %reshape.50), kind=kLoop, calls=%fused_computation.33 | loop fusion | bytes 6291456 | tf_op jit(solution)/shard_map/squeeze | solution.py:59
  98.9 2.6 %reshape_squeeze.3 = bf16[4,512,4,64]{1,0,3,2:T(4,128)(2,1)} reshape(bf16[2048,1,4,64]{0,3,2,1:T(8,128)(2,1)} %get-tuple-element.80) | data formatting | bytes 2097152 | tf_op jit(solution)/shard_map/reshape;squeeze | solution.py:33
  101.5 2.4 %copy.32 = bf16[4,512,4,64]{1,3,2,0:T(8,128)(2,1)} copy(bf16[4,512,4,64]{1,0,3,2:T(4,128)(2,1)} %reshape_squeeze.3) | data formatting | bytes 2097152 | tf_op jit(solution)/shard_map/while | solution.py:33
  103.9 3.8 %convolution_convert_fusion.1 = bf16[128,2048]{1,0:T(8,128)(2,1)} fusion(bf16[1024,2048]{1,0:T(8,128)(2,1)} %param.22, bf16[8,128,1024]{2,1,0:T(8,128)(2,1)} %all-gather.3.cloned.1.call-done, s32[]{:T(128)S(6)} %min.4, pred[]{:T(512)S(6)} %and.4), kind=kOutput, calls=%fused_computation.20 | convolution fusion | flops 537264128 | bytes 4980741 | tf_op jit(solution)/shard_map/dot_general | solution.py:69
  107.7 0.0 all-gather.5.cloned.1.call-update
  107.8 0.0 copy-start.9
  107.8 33.5 %while.2 = (s32[]{:T(128)}, bf16[4,512,4,64]{1,3,2,0:T(8,128)(2,1)}, bf16[4,512,4,64]{1,3,2,0:T(8,128)(2,1)}, bf16[2048,4,64]{0,2,1:T(8,128)(2,1)S(1)}, bf16[2048,4,64]{0,2,1:T(8,128)(2,1)}, /*index=5*/s32[]{:T(128)}) while((s32[]{:T(128)}, bf16[4,512,4,64]{1,3,2,0:T(8,128)(2,1)}, bf16[4,512,4,64]{1,3,2,0:T(8,128)(2,1)}, ...), condition=%wide.region_3.4_spmd, body=%wide.region_1.3_spmd.sunk | while | flops 1094842368 | bytes 40386672 | solution.py:33
  107.8 0.0 copy-start.4
  107.8 4.0 %fusion.49 = (f32[4,512]{1,0:T(4,128)S(1)}, f32[4,512,2048]{2,1,0:T(8,128)S(1)}) fusion(bf16[2048,4,64]{0,2,1:T(8,128)(2,1)S(1)} %get-tuple-element.135, bf16[4,512,4,64]{1,3,2,0:T(8,128)(2,1)} %get-tuple-element.134, s32[]{:T(128)S(6)} %copy.40), kind=kOutput, calls=%fused_computation.2.clone.1 | convolution fusion | flops 545257472 | bytes 18096132 | tf_op jit(solution)/shard_map/while/body/eval_jaxpr/qhd,khd->hqk/dot_general | solution.py:24
  111.8 0.0 copy-done.4
  111.9 4.3 %fusion.50 = bf16[4,512,4,64]{1,3,2,0:T(8,128)(2,1)} fusion(bf16[4,512,4,64]{1,3,2,0:T(8,128)(2,1)} %get-tuple-element.127, s32[]{:T(128)S(6)} %copy.40, bf16[2048,4,64]{0,2,1:T(8,128)(2,1)S(1)} %copy-done.4, f32[4,512,2048]{2,1,0:T(8,128)S(1)} %get-tuple-element.118, f32[4,512]{1,0:T(4,128)S(1)} %get-tuple-element.119), kind=kOutput, calls=%fused_computation.6.clone.1 | convolution fusion | flops 549584896 | bytes 18096132 | tf_op jit(solution)/shard_map/while/body/eval_jaxpr/hqk,khd->qhd/dot_general | solution.py:29
  116.2 4.1 %fusion.49 = (f32[4,512]{1,0:T(4,128)S(1)}, f32[4,512,2048]{2,1,0:T(8,128)S(1)}) fusion(bf16[2048,4,64]{0,2,1:T(8,128)(2,1)S(1)} %get-tuple-element.135, bf16[4,512,4,64]{1,3,2,0:T(8,128)(2,1)} %get-tuple-element.134, s32[]{:T(128)S(6)} %copy.40), kind=kOutput, calls=%fused_computation.2.clone.1 | convolution fusion | flops 545257472 | bytes 18096132 | tf_op jit(solution)/shard_map/while/body/eval_jaxpr/qhd,khd->hqk/dot_general | solution.py:24
  120.3 0.0 copy-done.4
  120.3 4.3 %fusion.50 = bf16[4,512,4,64]{1,3,2,0:T(8,128)(2,1)} fusion(bf16[4,512,4,64]{1,3,2,0:T(8,128)(2,1)} %get-tuple-element.127, s32[]{:T(128)S(6)} %copy.40, bf16[2048,4,64]{0,2,1:T(8,128)(2,1)S(1)} %copy-done.4, f32[4,512,2048]{2,1,0:T(8,128)S(1)} %get-tuple-element.118, f32[4,512]{1,0:T(4,128)S(1)} %get-tuple-element.119), kind=kOutput, calls=%fused_computation.6.clone.1 | convolution fusion | flops 549584896 | bytes 18096132 | tf_op jit(solution)/shard_map/while/body/eval_jaxpr/hqk,khd->qhd/dot_general | solution.py:29
  124.6 4.0 %fusion.49 = (f32[4,512]{1,0:T(4,128)S(1)}, f32[4,512,2048]{2,1,0:T(8,128)S(1)}) fusion(bf16[2048,4,64]{0,2,1:T(8,128)(2,1)S(1)} %get-tuple-element.135, bf16[4,512,4,64]{1,3,2,0:T(8,128)(2,1)} %get-tuple-element.134, s32[]{:T(128)S(6)} %copy.40), kind=kOutput, calls=%fused_computation.2.clone.1 | convolution fusion | flops 545257472 | bytes 18096132 | tf_op jit(solution)/shard_map/while/body/eval_jaxpr/qhd,khd->hqk/dot_general | solution.py:24
  128.6 4.3 %fusion.50 = bf16[4,512,4,64]{1,3,2,0:T(8,128)(2,1)} fusion(bf16[4,512,4,64]{1,3,2,0:T(8,128)(2,1)} %get-tuple-element.127, s32[]{:T(128)S(6)} %copy.40, bf16[2048,4,64]{0,2,1:T(8,128)(2,1)S(1)} %copy-done.4, f32[4,512,2048]{2,1,0:T(8,128)S(1)} %get-tuple-element.118, f32[4,512]{1,0:T(4,128)S(1)} %get-tuple-element.119), kind=kOutput, calls=%fused_computation.6.clone.1 | convolution fusion | flops 549584896 | bytes 18096132 | tf_op jit(solution)/shard_map/while/body/eval_jaxpr/hqk,khd->qhd/dot_general | solution.py:29
  132.9 4.0 %fusion.49 = (f32[4,512]{1,0:T(4,128)S(1)}, f32[4,512,2048]{2,1,0:T(8,128)S(1)}) fusion(bf16[2048,4,64]{0,2,1:T(8,128)(2,1)S(1)} %get-tuple-element.135, bf16[4,512,4,64]{1,3,2,0:T(8,128)(2,1)} %get-tuple-element.134, s32[]{:T(128)S(6)} %copy.40), kind=kOutput, calls=%fused_computation.2.clone.1 | convolution fusion | flops 545257472 | bytes 18096132 | tf_op jit(solution)/shard_map/while/body/eval_jaxpr/qhd,khd->hqk/dot_general | solution.py:24
  137.0 0.0 copy-done.4
  137.0 4.3 %fusion.50 = bf16[4,512,4,64]{1,3,2,0:T(8,128)(2,1)} fusion(bf16[4,512,4,64]{1,3,2,0:T(8,128)(2,1)} %get-tuple-element.127, s32[]{:T(128)S(6)} %copy.40, bf16[2048,4,64]{0,2,1:T(8,128)(2,1)S(1)} %copy-done.4, f32[4,512,2048]{2,1,0:T(8,128)S(1)} %get-tuple-element.118, f32[4,512]{1,0:T(4,128)S(1)} %get-tuple-element.119), kind=kOutput, calls=%fused_computation.6.clone.1 | convolution fusion | flops 549584896 | bytes 18096132 | tf_op jit(solution)/shard_map/while/body/eval_jaxpr/hqk,khd->qhd/dot_general | solution.py:29
  141.3 3.7 %all-to-all-start.1 = ((bf16[4,512,256]{1,2,0:T(8,128)(2,1)}), bf16[4,512,256]{1,2,0:T(8,128)(2,1)S(1)}, u32[]{:S(2)}, u32[]{:S(2)}) async-start(bf16[4,512,256]{1,2,0:T(8,128)(2,1)} %bitcast.80), calls=%async_computation.1 | async-start | bytes 2097152 | tf_op jit(solution)/shard_map/all_to_all | solution.py:60
  146.7 0.6 dynamic_slice.20
  147.3 0.6 iota_compare_fusion
  148.0 11.3 %all-to-all-done.1 = bf16[4,512,256]{1,2,0:T(8,128)(2,1)S(1)} async-done(((bf16[4,512,256]{1,2,0:T(8,128)(2,1)}), bf16[4,512,256]{1,2,0:T(8,128)(2,1)S(1)}, u32[]{:S(2)}, u32[]{:S(2)}) %all-to-all-start.1) | async-done | bytes 1048608 | tf_op jit(solution)/shard_map/all_to_all | solution.py:60
  159.2 2.7 %multiply_reduce_fusion = (f32[512]{0:T(512)S(1)}, f32[512,1024]{1,0:T(8,128)S(1)}) fusion(bf16[512,1024]{0,1:T(8,128)(2,1)S(1)} %bitcast.77, bf16[1024,1024]{1,0:T(8,128)(2,1)S(1)} %copy-done, bf16[1,512,1024]{2,1,0:T(8,128)(2,1)} %param.13), kind=kOutput, calls=%fused_computation.26 | convolution fusion | flops 1075838464 | bytes 6293504 | tf_op jit(solution)/shard_map/dot_general | solution.py:61
  162.0 1.3 copy-done.1
  163.3 2.3 %convolution_convert_fusion.2 = bf16[512,1024]{1,0:T(8,128)(2,1)} fusion(bf16[1024,1024]{1,0:T(8,128)(2,1)S(1)} %copy-done.5, f32[512,1024]{1,0:T(8,128)S(1)} %get-tuple-element.82, f32[1024]{0:T(1024)S(1)} %copy-done.7, f32[512]{0:T(512)S(1)} %add_rsqrt_fusion), kind=kOutput, calls=%fused_computation.28 | convolution fusion | flops 1075838976 | bytes 5249024 | tf_op jit(solution)/shard_map/dot_general | solution.py:63
  165.6 1.5 copy.34
  167.1 0.0 all-gather.5.cloned.1.call-done
  167.1 3.9 %copy.33 = bf16[512,2048]{0,1:T(8,128)(2,1)} copy(bf16[512,2048]{1,0:T(8,128)(2,1)} %all-gather.5.cloned.1.call-done) | data formatting | bytes 4194304 | tf_op jit(solution)/shard_map/all_gather | solution.py:70
  171.0 5.5 %fusion.10 = (f32[16,512]{1,0:T(8,128)S(1)}, f32[16,512,512]{1,2,0:T(8,128)S(1)}) fusion(pred[512]{0:T(512)(128)(4,1)S(1)} %iota_compare_fusion, bf16[512,16,64]{0,2,1:T(8,128)(2,1)S(1)} %bitcast.81, bf16[512,2,16,64]{0,3,2,1:T(8,128)(2,1)} %bitcast.78), kind=kOutput, calls=%fused_computation.14 | convolution fusion | flops 549445632 | bytes 18907648 | tf_op jit(solution)/shard_map/while/body/eval_jaxpr/qhd,khd->hqk/dot_general | solution.py:24
  176.6 0.0 copy-start.6
  176.6 3.7 %fusion.15 = bf16[16,64,512]{2,1,0:T(8,128)(2,1)S(1)} fusion(f32[16,512,512]{1,2,0:T(8,128)S(1)} %get-tuple-element.84, f32[16,512]{1,0:T(8,128)S(1)} %get-tuple-element.83, pred[512]{0:T(512)(128)(4,1)S(1)} %iota_compare_fusion, bf16[512,2,16,64]{0,3,2,1:T(8,128)(2,1)S(1)} %bitcast.79), kind=kOutput, calls=%fused_computation.27 | convolution fusion | flops 554172416 | bytes 18907648 | tf_op jit(solution)/shard_map/while/body/eval_jaxpr/hqk,khd->qhd/dot_general | solution.py:29
  180.4 2.2 %fusion.16 = bf16[1,512,1024]{2,1,0:T(8,128)(2,1)} fusion(f32[512,1024]{1,0:T(8,128)S(1)} %copy-done.2, bf16[512,1024]{0,1:T(8,128)(2,1)S(1)} %bitcast.82, bf16[1024,1024]{1,0:T(8,128)(2,1)S(1)} %copy-done.6), kind=kOutput, calls=%fused_computation.29 | convolution fusion | flops 1074790400 | bytes 6291456 | tf_op jit(solution)/shard_map/dot_general | solution.py:76
  (21 shorter events, 0.0 us)
Async XLA Ops:
  6.5 152.7 %copy-start = (bf16[1024,1024]{1,0:T(8,128)(2,1)S(1)}, bf16[1024,1024]{1,0:T(8,128)(2,1)}, u32[]{:S(2)}) copy-start(bf16[1024,1024]{1,0:T(8,128)(2,1)} %param.19) | copy-start | bytes 6291460
  6.5 97.4 %all-gather.3.cloned.1.call-start = ((), (), s32[]{:S(2)}) async-start(), calls=%async_computation.2 | async-start | bytes 2359296 | tf_op jit(solution)/shard_map/all_gather | solution.py:68
  28.3 5.2 %copy-start.8 = (s32[8]{0:T(128)S(1)}, s32[8]{0:T(128)}, u32[]{:S(2)}) copy-start(s32[8]{0:T(128)} %param.16) | copy-start | bytes 100
  28.3 53.9 %all-to-all-start = ((bf16[512,3,1024]{0,1,2:T(4,128)(2,1)}), bf16[512,3,1024]{0,1,2:T(4,128)(2,1)}, u32[]{:S(2)}, u32[]{:S(2)}) async-start(bf16[512,3,1024]{0,1,2:T(4,128)(2,1)} %copy.29), calls=%async_computation | async-start | bytes 8388608 | tf_op jit(solution)/shard_map/all_to_all | solution.py:55
  33.3 133.8 %all-gather.5.cloned.1.call-start = ((), (), s32[]{:S(2)}) async-start(), calls=%async_computation.3 | async-start | bytes 2621440 | tf_op jit(solution)/shard_map/all_gather | solution.py:70
  107.8 38.9 %copy-start.9 = (s32[8]{0:T(128)S(1)}, s32[8]{0:T(128)}, u32[]{:S(2)}) copy-start(s32[8]{0:T(128)} %param.15) | copy-start | bytes 100
  107.8 4.1 %copy-start.4 = (bf16[2048,4,64]{0,2,1:T(8,128)(2,1)S(1)}, bf16[2048,4,64]{0,2,1:T(8,128)(2,1)}, u32[]{:S(2)}) copy-start(bf16[2048,4,64]{0,2,1:T(8,128)(2,1)} %get-tuple-element.136) | copy-start | bytes 3145732 | tf_op jit(solution)/shard_map/while
  116.2 4.1 %copy-start.4 = (bf16[2048,4,64]{0,2,1:T(8,128)(2,1)S(1)}, bf16[2048,4,64]{0,2,1:T(8,128)(2,1)}, u32[]{:S(2)}) copy-start(bf16[2048,4,64]{0,2,1:T(8,128)(2,1)} %get-tuple-element.136) | copy-start | bytes 3145732 | tf_op jit(solution)/shard_map/while
  124.6 4.0 %copy-start.4 = (bf16[2048,4,64]{0,2,1:T(8,128)(2,1)S(1)}, bf16[2048,4,64]{0,2,1:T(8,128)(2,1)}, u32[]{:S(2)}) copy-start(bf16[2048,4,64]{0,2,1:T(8,128)(2,1)} %get-tuple-element.136) | copy-start | bytes 3145732 | tf_op jit(solution)/shard_map/while
  132.9 4.0 %copy-start.4 = (bf16[2048,4,64]{0,2,1:T(8,128)(2,1)S(1)}, bf16[2048,4,64]{0,2,1:T(8,128)(2,1)}, u32[]{:S(2)}) copy-start(bf16[2048,4,64]{0,2,1:T(8,128)(2,1)} %get-tuple-element.136) | copy-start | bytes 3145732 | tf_op jit(solution)/shard_map/while
  141.3 18.0 %all-to-all-start.1 = ((bf16[4,512,256]{1,2,0:T(8,128)(2,1)}), bf16[4,512,256]{1,2,0:T(8,128)(2,1)S(1)}, u32[]{:S(2)}, u32[]{:S(2)}) async-start(bf16[4,512,256]{1,2,0:T(8,128)(2,1)} %bitcast.80), calls=%async_computation.1 | async-start | bytes 2097152 | tf_op jit(solution)/shard_map/all_to_all | solution.py:60
  159.2 4.1 %copy-start.5 = (bf16[1024,1024]{1,0:T(8,128)(2,1)S(1)}, bf16[1024,1024]{1,0:T(8,128)(2,1)}, u32[]{:S(2)}) copy-start(bf16[1024,1024]{1,0:T(8,128)(2,1)} %param.21) | copy-start | bytes 6291460
  159.2 4.1 %copy-start.7 = (f32[1024]{0:T(1024)S(1)}, f32[1024]{0:T(1024)}, u32[]{:S(2)}) copy-start(f32[1024]{0:T(1024)} %param.20) | copy-start | bytes 12292
  162.0 1.3 copy-start.1
  171.0 5.5 %copy-start.3 = (bf16[512,2048]{0,1:T(8,128)(2,1)S(1)}, bf16[512,2048]{0,1:T(8,128)(2,1)}, u32[]{:S(2)}) copy-start(bf16[512,2048]{0,1:T(8,128)(2,1)} %copy.33) | copy-start | bytes 6291460
  176.6 3.8 %copy-start.2 = (f32[512,1024]{1,0:T(8,128)S(1)}, f32[512,1024]{1,0:T(8,128)}, u32[]{:S(2)}) copy-start(f32[512,1024]{1,0:T(8,128)} %copy-done.1) | copy-start | bytes 6291460
  176.6 3.8 %copy-start.6 = (bf16[1024,1024]{1,0:T(8,128)(2,1)S(1)}, bf16[1024,1024]{1,0:T(8,128)(2,1)}, u32[]{:S(2)}) copy-start(bf16[1024,1024]{1,0:T(8,128)(2,1)} %param.23) | copy-start | bytes 6291460
Sparse Core Ops, SparseCore 0:
  9.5 51.9 all-gather.2
  107.9 23.6 all-gather.4
where the time goes:
time: 190 us; the launch traced here: 189 us
  matrix products  62 us (33%)
  waiting for transfers between devices  58.4 us (31%)
  local copies, waits for them, and re-layouts  41 us (22%)
  between operations  16.9 us (9%)
  starting transfers between devices  8.93 us (5%)
  other arithmetic  2.16 us (1%)
    all_to_all x1, waiting for transfers between devices, per_device(): lax.all_to_all(stacked, 'seq', split_axis=2, concat_axis=0, tiled=True)  46.4 us
    dot_general x5, matrix products, one_block(): jnp.einsum('qhd,khd->hqk', query_block, keys, preferred_element_type=jnp....  21.7 us
    dot_general x5, matrix products, one_block(): jnp.einsum('hqk,khd->qhd', weights, values, preferred_element_type=jnp.fl...  20.9 us
    all_to_all x1, waiting for transfers between devices, per_device(): lax.all_to_all(attended, 'seq', split_axis=0, concat_axis=1, tiled=True)  11.3 us
    dot_general x1, matrix products, per_device(): jnp.dot(normed, w_qkv, preferred_element_type=jnp.float32)  8.28 us
    all_to_all x2, local copies, waits for them, and re-layouts, per_device(): lax.all_to_all(stacked, 'seq', split_axis=2, concat_axis=0, tiled=True)  7.07 us
    reshape x1, local copies, waits for them, and re-layouts, per_device(): stacked = projected.reshape(tok_rows, 3, D)  6.53 us
    reshape x1, local copies, waits for them, and re-layouts, per_device(): split = local_heads.reshape(seq_rows, 3, head_count, HEAD_DIM)  6.1 us
  transfers between devices with their start and end apart: 4, of which 2 were waited for; matrix products, arithmetic and copies ran while one was open for 45% of the time, Pallas kernels for 0%

commit v1 on v0

--- a/solution.py
+++ b/solution.py
@@ -6,6 +6,13 @@
 D = 1024
 HEADS = 16
 HEAD_DIM = 64
+
+
+def results_show(block_here, axis_no):
+    step_out = list(block_here.shape[1:])
+    step_out[axis_no] *= block_here.shape[0]
+    high = jnp.moveaxis(block_here, 0, axis_no).reshape(step_out)
+    return high
 
 
 def normalize(values, gain):
@@ -67,7 +74,27 @@
     empty = jnp.zeros(eq_embed.shape[1:], jnp.bfloat16)
     owned_rows = pick_slot(slot, empty, lax.all_gather(eq_embed, "dp", axis=0, tiled=True))
     owned_kv = jnp.dot(owned_rows, w_ckv, preferred_element_type=jnp.float32).astype(jnp.bfloat16)
-    whole_kv = lax.all_gather(owned_kv, "seq", axis=0, tiled=True)
+    parts_n = lax.axis_size("seq")
+    queue = []
+    for k in range(parts_n):
+        queue.append((k, (k + 1) % parts_n))
+    all_blocks = []
+    for j, idx in queue:
+        all_blocks.append((idx, j))
+    even, block_out = ([], [])
+    for i0 in range(parts_n - 1):
+        if i0 % 2 == 0:
+            even.append(lax.ppermute(even[-1] if even else owned_kv, axis_name="seq", perm=queue))
+        else:
+            block_out.append(
+                lax.ppermute(
+                    block_out[-1] if block_out else owned_kv, axis_name="seq", perm=all_blocks
+                )
+            )
+    mat_out = jnp.stack([*even[::-1], owned_kv, *block_out], axis=0)
+    v_next = lax.axis_index("seq") - len(even)
+    mat_out = mat_out[(jnp.arange(parts_n) - v_next) % parts_n]
+    whole_kv = results_show(mat_out, 0)
     whole_kv = whole_kv.reshape(eq_rows * groups, 2, HEADS, HEAD_DIM)
     valid = jnp.arange(eq_rows * groups, dtype=jnp.int32) < length
     cross_att = attend(

time: 190 us -> 207 us (1.089)
  local copies, waits for them, and re-layouts: 41 us -> 47.9 us
  waiting for transfers between devices: 58.4 us -> 63.1 us
  other arithmetic: 2.16 us -> 5.48 us
    ppermute x0 -> x3, waiting for transfers between devices: none -> 10 us  [the longest x2 5.75 us: per_device(): lax.ppermute(even[-1] if even else owned_kv, axis_name='seq', perm=queue)]
    gather x0 -> x2, local copies, waits for them, and re-layouts: none -> 7.85 us  [per_device(): mat_out = mat_out[(jnp.arange(parts_n) - v_next) % parts_n]]
    all_to_all x1, waiting for transfers between devices: 11.3 us -> 4.39 us  [per_device(): lax.all_to_all(attended, 'seq', split_axis=0, concat_axis=1, tiled=True)]
    another operation x0 -> x1, local copies, waits for them, and re-layouts: none -> 4.13 us  [per_device(): whole_kv = whole_kv.reshape(eq_rows * groups, 2, HEADS, HEAD_DIM)]
    all_gather x1 -> x0, local copies, waits for them, and re-layouts: 3.93 us -> none  [per_device(): whole_kv = lax.all_gather(owned_kv, 'seq', axis=0, tiled=True)]
    another operation x0 -> x1, other arithmetic: none -> 3.1 us  [per_device(): mat_out = jnp.stack([*even[::-1], owned_kv, *block_out], axis=0)]
  transfers between devices with their start and end apart: 4 -> 6, of which waited for: 2 -> 5; matrix products, arithmetic and copies ran while one was open for 45% -> 33% of each run, Pallas kernels for 0% -> 0%
where the time goes in v1:
time: 207 us; the launch traced here: 206 us
  waiting for transfers between devices  63.1 us (30%)
  matrix products  62 us (30%)
  local copies, waits for them, and re-layouts  47.9 us (23%)
  between operations  17.7 us (9%)
  starting transfers between devices  9.95 us (5%)
  other arithmetic  5.48 us (3%)
    all_to_all x1, waiting for transfers between devices, per_device(): lax.all_to_all(stacked, 'seq', split_axis=2, concat_axis=0, tiled=True)  48.2 us
    dot_general x5, matrix products, one_block(): jnp.einsum('qhd,khd->hqk', query_block, keys, preferred_element_type=jnp....  21.6 us
    dot_general x5, matrix products, one_block(): jnp.einsum('hqk,khd->qhd', weights, values, preferred_element_type=jnp.fl...  20.9 us
    dot_general x1, matrix products, per_device(): jnp.dot(normed, w_qkv, preferred_element_type=jnp.float32)  8.28 us
    gather x2, local copies, waits for them, and re-layouts, per_device(): mat_out = mat_out[(jnp.arange(parts_n) - v_next) % parts_n]  7.85 us
    all_to_all x2, local copies, waits for them, and re-layouts, per_device(): lax.all_to_all(stacked, 'seq', split_axis=2, concat_axis=0, tiled=True)  7.08 us
    reshape x1, local copies, waits for them, and re-layouts, per_device(): stacked = projected.reshape(tok_rows, 3, D)  6.53 us
    reshape x1, local copies, waits for them, and re-layouts, per_device(): split = local_heads.reshape(seq_rows, 3, head_count, HEAD_DIM)  6.1 us
  transfers between devices with their start and end apart: 6, of which 5 were waited for; matrix products, arithmetic and copies ran while one was open for 33% of the time, Pallas kernels for 0%

profile of v1, /device:TPU:0, one launch (start us, length us, event | category | flops | bytes accessed | tf_op | source)
XLA Modules:
  0.0 206.2 jit_solution(17085178562978198239)
XLA Ops:
  6.5 1.7 fusion.12
  8.2 8.3 %convolution_convert_fusion = bf16[512,3072]{1,0:T(8,128)(2,1)} fusion(bf16[1024,3072]{1,0:T(8,128)(2,1)} %param.18, bf16[1,512,1024]{2,1,0:T(8,128)(2,1)} %param.13, f32[1024]{0:T(1024)} %param.17, f32[512]{0:T(512)S(1)} %add_rsqrt_fusion.1), kind=kOutput, calls=%fused_computation.17 | convolution fusion | flops 3224895488 | bytes 10491904 | tf_op jit(solution)/shard_map/dot_general | solution.py:60
  16.5 4.7 %copy.28 = bf16[512,3072]{0,1:T(8,128)(2,1)} copy(bf16[512,3072]{1,0:T(8,128)(2,1)} %convolution_convert_fusion) | data formatting | bytes 6291456 | tf_op jit(solution)/shard_map/convert_element_type | solution.py:60
  21.1 6.5 %copy.29 = bf16[512,3,1024]{0,1,2:T(4,128)(2,1)} copy(bf16[512,3,1024]{0,2,1:T(8,128)(2,1)} %bitcast.82) | data formatting | bytes 6291456 | tf_op jit(solution)/shard_map/reshape | solution.py:61
  27.7 4.8 %all-to-all-start = ((bf16[512,3,1024]{0,1,2:T(4,128)(2,1)}), bf16[512,3,1024]{0,1,2:T(4,128)(2,1)}, u32[]{:S(2)}, u32[]{:S(2)}) async-start(bf16[512,3,1024]{0,1,2:T(4,128)(2,1)} %copy.29), calls=%async_computation | async-start | bytes 8388608 | tf_op jit(solution)/shard_map/all_to_all | solution.py:62
  32.5 0.2 all-gather.2.cloned.1.call-start
  32.8 0.5 all-gather.2.cloned.1.call-update
  33.3 48.2 %all-to-all-done = bf16[512,3,1024]{0,1,2:T(4,128)(2,1)} async-done(((bf16[512,3,1024]{0,1,2:T(4,128)(2,1)}), bf16[512,3,1024]{0,1,2:T(4,128)(2,1)}, u32[]{:S(2)}, u32[]{:S(2)}) %all-to-all-start) | async-done | bytes 3145760 | tf_op jit(solution)/shard_map/all_to_all | solution.py:62
  81.4 3.0 %copy.30 = bf16[512,3,1024]{0,2,1:T(8,128)(2,1)S(1)} copy(bf16[512,3,1024]{0,1,2:T(4,128)(2,1)} %all-to-all-done) | data formatting | bytes 6291456 | tf_op jit(solution)/shard_map/all_to_all | solution.py:62
  84.4 4.1 %copy.31 = bf16[4,512,3,256]{1,0,3,2:T(4,128)(2,1)} copy(bf16[4,512,3,256]{1,3,0,2:T(8,128)(2,1)S(1)} %bitcast.83) | data formatting | bytes 6291456 | tf_op jit(solution)/shard_map/all_to_all | solution.py:62
  88.5 6.1 %reshape.96 = bf16[2048,3,4,64]{0,3,2,1:T(8,128)(2,1)} reshape(bf16[4,512,3,256]{1,0,3,2:T(4,128)(2,1)} %copy.31) | data formatting | bytes 6291456 | tf_op jit(solution)/shard_map/reshape | solution.py:64
  94.6 3.6 %slice_bitcast_fusion.4 = (bf16[2048,4,64]{0,2,1:T(8,128)(2,1)}, bf16[2048,4,64]{0,2,1:T(8,128)(2,1)S(1)}, bf16[2048,1,4,64]{0,3,2,1:T(8,128)(2,1)}) fusion(bf16[2048,3,4,64]{0,3,2,1:T(8,128)(2,1)} %reshape.96), kind=kLoop, calls=%fused_computation.35 | loop fusion | bytes 6291456 | tf_op jit(solution)/shard_map/squeeze | solution.py:66
  98.2 2.6 %reshape_squeeze.3 = bf16[4,512,4,64]{1,0,3,2:T(4,128)(2,1)} reshape(bf16[2048,1,4,64]{0,3,2,1:T(8,128)(2,1)} %get-tuple-element.80) | data formatting | bytes 2097152 | tf_op jit(solution)/shard_map/reshape;squeeze | solution.py:40
  100.8 2.4 %copy.32 = bf16[4,512,4,64]{1,3,2,0:T(8,128)(2,1)} copy(bf16[4,512,4,64]{1,0,3,2:T(4,128)(2,1)} %reshape_squeeze.3) | data formatting | bytes 2097152 | tf_op jit(solution)/shard_map/while | solution.py:40
  103.2 33.4 %while.2 = (s32[]{:T(128)}, bf16[4,512,4,64]{1,3,2,0:T(8,128)(2,1)}, bf16[4,512,4,64]{1,3,2,0:T(8,128)(2,1)}, bf16[2048,4,64]{0,2,1:T(8,128)(2,1)S(1)}, bf16[2048,4,64]{0,2,1:T(8,128)(2,1)}, /*index=5*/s32[]{:T(128)}) while((s32[]{:T(128)}, bf16[4,512,4,64]{1,3,2,0:T(8,128)(2,1)}, bf16[4,512,4,64]{1,3,2,0:T(8,128)(2,1)}, ...), condition=%wide.region_3.4_spmd, body=%wide.region_1.3_spmd.sunk | while | flops 1094842368 | bytes 40386672 | solution.py:40
  103.3 4.0 %fusion.51 = (f32[4,512]{1,0:T(4,128)S(1)}, f32[4,512,2048]{2,1,0:T(8,128)S(1)}) fusion(bf16[2048,4,64]{0,2,1:T(8,128)(2,1)S(1)} %get-tuple-element.135, bf16[4,512,4,64]{1,3,2,0:T(8,128)(2,1)} %get-tuple-element.134, s32[]{:T(128)S(6)} %copy.40), kind=kOutput, calls=%fused_computation.3.clone.1 | convolution fusion | flops 545257472 | bytes 18096132 | tf_op jit(solution)/shard_map/while/body/eval_jaxpr/qhd,khd->hqk/dot_general | solution.py:31
  107.3 4.3 %fusion.52 = bf16[4,512,4,64]{1,3,2,0:T(8,128)(2,1)} fusion(bf16[4,512,4,64]{1,3,2,0:T(8,128)(2,1)} %get-tuple-element.127, s32[]{:T(128)S(6)} %copy.40, bf16[2048,4,64]{0,2,1:T(8,128)(2,1)S(1)} %copy-done.5, f32[4,512,2048]{2,1,0:T(8,128)S(1)} %get-tuple-element.118, f32[4,512]{1,0:T(4,128)S(1)} %get-tuple-element.119), kind=kOutput, calls=%fused_computation.7.clone.1 | convolution fusion | flops 549584896 | bytes 18096132 | tf_op jit(solution)/shard_map/while/body/eval_jaxpr/hqk,khd->qhd/dot_general | solution.py:36
  111.6 4.0 %fusion.51 = (f32[4,512]{1,0:T(4,128)S(1)}, f32[4,512,2048]{2,1,0:T(8,128)S(1)}) fusion(bf16[2048,4,64]{0,2,1:T(8,128)(2,1)S(1)} %get-tuple-element.135, bf16[4,512,4,64]{1,3,2,0:T(8,128)(2,1)} %get-tuple-element.134, s32[]{:T(128)S(6)} %copy.40), kind=kOutput, calls=%fused_computation.3.clone.1 | convolution fusion | flops 545257472 | bytes 18096132 | tf_op jit(solution)/shard_map/while/body/eval_jaxpr/qhd,khd->hqk/dot_general | solution.py:31
  115.6 4.3 %fusion.52 = bf16[4,512,4,64]{1,3,2,0:T(8,128)(2,1)} fusion(bf16[4,512,4,64]{1,3,2,0:T(8,128)(2,1)} %get-tuple-element.127, s32[]{:T(128)S(6)} %copy.40, bf16[2048,4,64]{0,2,1:T(8,128)(2,1)S(1)} %copy-done.5, f32[4,512,2048]{2,1,0:T(8,128)S(1)} %get-tuple-element.118, f32[4,512]{1,0:T(4,128)S(1)} %get-tuple-element.119), kind=kOutput, calls=%fused_computation.7.clone.1 | convolution fusion | flops 549584896 | bytes 18096132 | tf_op jit(solution)/shard_map/while/body/eval_jaxpr/hqk,khd->qhd/dot_general | solution.py:36
  120.0 4.0 %fusion.51 = (f32[4,512]{1,0:T(4,128)S(1)}, f32[4,512,2048]{2,1,0:T(8,128)S(1)}) fusion(bf16[2048,4,64]{0,2,1:T(8,128)(2,1)S(1)} %get-tuple-element.135, bf16[4,512,4,64]{1,3,2,0:T(8,128)(2,1)} %get-tuple-element.134, s32[]{:T(128)S(6)} %copy.40), kind=kOutput, calls=%fused_computation.3.clone.1 | convolution fusion | flops 545257472 | bytes 18096132 | tf_op jit(solution)/shard_map/while/body/eval_jaxpr/qhd,khd->hqk/dot_general | solution.py:31
  124.0 4.3 %fusion.52 = bf16[4,512,4,64]{1,3,2,0:T(8,128)(2,1)} fusion(bf16[4,512,4,64]{1,3,2,0:T(8,128)(2,1)} %get-tuple-element.127, s32[]{:T(128)S(6)} %copy.40, bf16[2048,4,64]{0,2,1:T(8,128)(2,1)S(1)} %copy-done.5, f32[4,512,2048]{2,1,0:T(8,128)S(1)} %get-tuple-element.118, f32[4,512]{1,0:T(4,128)S(1)} %get-tuple-element.119), kind=kOutput, calls=%fused_computation.7.clone.1 | convolution fusion | flops 549584896 | bytes 18096132 | tf_op jit(solution)/shard_map/while/body/eval_jaxpr/hqk,khd->qhd/dot_general | solution.py:36
  128.3 4.0 %fusion.51 = (f32[4,512]{1,0:T(4,128)S(1)}, f32[4,512,2048]{2,1,0:T(8,128)S(1)}) fusion(bf16[2048,4,64]{0,2,1:T(8,128)(2,1)S(1)} %get-tuple-element.135, bf16[4,512,4,64]{1,3,2,0:T(8,128)(2,1)} %get-tuple-element.134, s32[]{:T(128)S(6)} %copy.40), kind=kOutput, calls=%fused_computation.3.clone.1 | convolution fusion | flops 545257472 | bytes 18096132 | tf_op jit(solution)/shard_map/while/body/eval_jaxpr/qhd,khd->hqk/dot_general | solution.py:31
  132.4 4.3 %fusion.52 = bf16[4,512,4,64]{1,3,2,0:T(8,128)(2,1)} fusion(bf16[4,512,4,64]{1,3,2,0:T(8,128)(2,1)} %get-tuple-element.127, s32[]{:T(128)S(6)} %copy.40, bf16[2048,4,64]{0,2,1:T(8,128)(2,1)S(1)} %copy-done.5, f32[4,512,2048]{2,1,0:T(8,128)S(1)} %get-tuple-element.118, f32[4,512]{1,0:T(4,128)S(1)} %get-tuple-element.119), kind=kOutput, calls=%fused_computation.7.clone.1 | convolution fusion | flops 549584896 | bytes 18096132 | tf_op jit(solution)/shard_map/while/body/eval_jaxpr/hqk,khd->qhd/dot_general | solution.py:36
  136.7 4.4 %all-to-all-start.1 = ((bf16[4,512,256]{1,2,0:T(8,128)(2,1)}), bf16[4,512,256]{1,2,0:T(8,128)(2,1)}, u32[]{:S(2)}, u32[]{:S(2)}) async-start(bf16[4,512,256]{1,2,0:T(8,128)(2,1)} %bitcast.84), calls=%async_computation.1 | async-start | bytes 2097152 | tf_op jit(solution)/shard_map/all_to_all | solution.py:67
  141.1 0.7 dynamic_slice.18
  145.9 0.7 dynamic_slice.20
  146.6 0.0 copy-start.1
  146.6 0.0 all-gather.2.cloned.1.call-done
  146.6 3.9 %convolution_convert_fusion.1 = bf16[128,2048]{1,0:T(8,128)(2,1)} fusion(bf16[1024,2048]{1,0:T(8,128)(2,1)} %param.22, bf16[8,128,1024]{2,1,0:T(8,128)(2,1)} %all-gather.2.cloned.1.call-done, s32[]{:T(128)S(6)} %min.4, pred[]{:T(512)S(6)} %and.23), kind=kOutput, calls=%fused_computation.21 | convolution fusion | flops 537264128 | bytes 4980741 | tf_op jit(solution)/shard_map/dot_general | solution.py:76
  150.5 0.4 collective-permute-start
  150.9 0.7 iota_compare_fusion
  151.6 4.4 %all-to-all-done.1 = bf16[4,512,256]{1,2,0:T(8,128)(2,1)} async-done(((bf16[4,512,256]{1,2,0:T(8,128)(2,1)}), bf16[4,512,256]{1,2,0:T(8,128)(2,1)}, u32[]{:S(2)}, u32[]{:S(2)}) %all-to-all-start.1) | async-done | bytes 1048608 | tf_op jit(solution)/shard_map/all_to_all | solution.py:67
  156.1 2.7 %multiply_reduce_fusion = (f32[512]{0:T(512)S(1)}, f32[512,1024]{1,0:T(8,128)S(1)}) fusion(bf16[512,1024]{0,1:T(8,128)(2,1)} %bitcast.12, bf16[1024,1024]{1,0:T(8,128)(2,1)S(1)} %copy-done, bf16[1,512,1024]{2,1,0:T(8,128)(2,1)S(1)} %copy-done.1), kind=kOutput, calls=%fused_computation.28 | convolution fusion | flops 1075838464 | bytes 6293504 | tf_op jit(solution)/shard_map/dot_general | solution.py:68
  158.8 0.1 collective-permute-start.2
  158.9 2.3 %collective-permute-done = bf16[128,2048]{1,0:T(8,128)(2,1)} collective-permute-done((bf16[128,2048]{1,0:T(8,128)(2,1)}, bf16[128,2048]{1,0:T(8,128)(2,1)}, u32[]{:S(2)}, u32[]{:S(2)}) %collective-permute-start) | collective-permute-done | bytes 524320 | tf_op jit(solution)/shard_map/ppermute | solution.py:87
  161.2 0.0 collective-permute-start.1
  161.2 2.3 %convolution_convert_fusion.2 = bf16[512,1024]{1,0:T(8,128)(2,1)} fusion(bf16[1024,1024]{1,0:T(8,128)(2,1)S(1)} %copy-done.6, f32[512,1024]{1,0:T(8,128)S(1)} %get-tuple-element.82, f32[1024]{0:T(1024)S(1)} %copy-done.8, f32[512]{0:T(512)S(1)} %add_rsqrt_fusion), kind=kOutput, calls=%fused_computation.30 | convolution fusion | flops 1075838976 | bytes 5249024 | tf_op jit(solution)/shard_map/dot_general | solution.py:70
  163.5 1.5 copy.34
  165.0 4.3 %collective-permute-done.2 = bf16[128,2048]{1,0:T(8,128)(2,1)} collective-permute-done((bf16[128,2048]{1,0:T(8,128)(2,1)}, bf16[128,2048]{1,0:T(8,128)(2,1)}, u32[]{:S(2)}, u32[]{:S(2)}) %collective-permute-start.2) | collective-permute-done | bytes 524320 | tf_op jit(solution)/shard_map/ppermute | solution.py:90
  169.3 3.4 %collective-permute-done.1 = bf16[128,2048]{1,0:T(8,128)(2,1)} collective-permute-done((bf16[128,2048]{1,0:T(8,128)(2,1)}, bf16[128,2048]{1,0:T(8,128)(2,1)}, u32[]{:S(2)}, u32[]{:S(2)}) %collective-permute-start.1) | collective-permute-done | bytes 524320 | tf_op jit(solution)/shard_map/ppermute | solution.py:87
  172.7 3.1 %pad_maximum_fusion = bf16[4,128,2048]{2,1,0:T(8,128)(2,1)} fusion(bf16[1,128,2048]{2,1,0:T(8,128)(2,1)} %bitcast.18, bf16[1,128,2048]{2,1,0:T(8,128)(2,1)} %bitcast.17, bf16[1,128,2048]{2,1,0:T(8,128)(2,1)} %bitcast.16, bf16[1,128,2048]{2,1,0:T(8,128)(2,1)} %bitcast.15), kind=kLoop, calls=%fused_computation.25 | loop fusion | flops 3145728 | bytes 4194304 | tf_op jit(solution)/shard_map/stack | solution.py:94
  175.8 3.6 %gather_fusion = bf16[4,128,2048]{2,1,0:T(8,128)(2,1)} fusion(bf16[4,128,2048]{2,1,0:T(8,128)(2,1)} %pad_maximum_fusion, s32[1024]{0:T(1024)S(1)} %pad_clamp_fusion), kind=kCustom, calls=%fused_computation | custom fusion | bytes 4194320 | tf_op jit(solution)/shard_map/gather | solution.py:96
  179.4 4.2 %copy.33 = bf16[4,128,2048]{1,0,2:T(4,128)(2,1)} copy(bf16[4,128,2048]{2,1,0:T(8,128)(2,1)} %gather_fusion) | data formatting | bytes 4194304 | tf_op jit(solution)/shard_map/gather | solution.py:96
  183.7 4.1 %reshape_reshape.4 = bf16[512,2,16,64]{0,3,2,1:T(8,128)(2,1)} reshape(bf16[4,128,2048]{1,0,2:T(4,128)(2,1)} %copy.33) | data formatting | bytes 4194304 | tf_op jit(solution)/shard_map/reshape;reshape | solution.py:98
  187.8 5.5 %fusion.10 = (f32[16,512]{1,0:T(8,128)S(1)}, f32[16,512,512]{1,2,0:T(8,128)S(1)}) fusion(pred[512]{0:T(512)(128)(4,1)S(1)} %iota_compare_fusion, bf16[512,16,64]{0,2,1:T(8,128)(2,1)S(1)} %bitcast.85, bf16[512,2,16,64]{0,3,2,1:T(8,128)(2,1)} %reshape_reshape.4), kind=kOutput, calls=%fused_computation.15 | convolution fusion | flops 549445632 | bytes 18907648 | tf_op jit(solution)/shard_map/while/body/eval_jaxpr/qhd,khd->hqk/dot_general | solution.py:31
  193.4 0.0 copy-start.7
  193.4 3.7 %fusion.15 = bf16[16,64,512]{2,1,0:T(8,128)(2,1)S(1)} fusion(f32[16,512,512]{1,2,0:T(8,128)S(1)} %get-tuple-element.84, f32[16,512]{1,0:T(8,128)S(1)} %get-tuple-element.83, pred[512]{0:T(512)(128)(4,1)S(1)} %iota_compare_fusion, bf16[512,2,16,64]{0,3,2,1:T(8,128)(2,1)S(1)} %copy-done.4), kind=kOutput, calls=%fused_computation.29 | convolution fusion | flops 554172416 | bytes 18907648 | tf_op jit(solution)/shard_map/while/body/eval_jaxpr/hqk,khd->qhd/dot_general | solution.py:36
  197.1 2.2 %fusion.16 = bf16[1,512,1024]{2,1,0:T(8,128)(2,1)} fusion(f32[512,1024]{1,0:T(8,128)S(1)} %copy-done.3, bf16[512,1024]{0,1:T(8,128)(2,1)S(1)} %bitcast.86, bf16[1024,1024]{1,0:T(8,128)(2,1)S(1)} %copy-done.7), kind=kOutput, calls=%fused_computation.31 | convolution fusion | flops 1074790400 | bytes 6291456 | tf_op jit(solution)/shard_map/dot_general | solution.py:103
  (31 shorter events, 0.1 us)
Async XLA Ops:
  6.5 149.5 %copy-start = (bf16[1024,1024]{1,0:T(8,128)(2,1)S(1)}, bf16[1024,1024]{1,0:T(8,128)(2,1)}, u32[]{:S(2)}) copy-start(bf16[1024,1024]{1,0:T(8,128)(2,1)} %param.19) | copy-start | bytes 6291460
  27.7 53.8 %all-to-all-start = ((bf16[512,3,1024]{0,1,2:T(4,128)(2,1)}), bf16[512,3,1024]{0,1,2:T(4,128)(2,1)}, u32[]{:S(2)}, u32[]{:S(2)}) async-start(bf16[512,3,1024]{0,1,2:T(4,128)(2,1)} %copy.29), calls=%async_computation | async-start | bytes 8388608 | tf_op jit(solution)/shard_map/all_to_all | solution.py:62
  32.5 114.1 %all-gather.2.cloned.1.call-start = ((), (), s32[]{:S(2)}) async-start(), calls=%async_computation.2 | async-start | bytes 2359296 | tf_op jit(solution)/shard_map/all_gather | solution.py:75
  103.2 4.0 %copy-start.5 = (bf16[2048,4,64]{0,2,1:T(8,128)(2,1)S(1)}, bf16[2048,4,64]{0,2,1:T(8,128)(2,1)}, u32[]{:S(2)}) copy-start(bf16[2048,4,64]{0,2,1:T(8,128)(2,1)} %get-tuple-element.136) | copy-start | bytes 3145732 | tf_op jit(solution)/shard_map/while
  111.6 4.0 %copy-start.5 = (bf16[2048,4,64]{0,2,1:T(8,128)(2,1)S(1)}, bf16[2048,4,64]{0,2,1:T(8,128)(2,1)}, u32[]{:S(2)}) copy-start(bf16[2048,4,64]{0,2,1:T(8,128)(2,1)} %get-tuple-element.136) | copy-start | bytes 3145732 | tf_op jit(solution)/shard_map/while
  119.9 4.0 %copy-start.5 = (bf16[2048,4,64]{0,2,1:T(8,128)(2,1)S(1)}, bf16[2048,4,64]{0,2,1:T(8,128)(2,1)}, u32[]{:S(2)}) copy-start(bf16[2048,4,64]{0,2,1:T(8,128)(2,1)} %get-tuple-element.136) | copy-start | bytes 3145732 | tf_op jit(solution)/shard_map/while
  128.3 4.0 %copy-start.5 = (bf16[2048,4,64]{0,2,1:T(8,128)(2,1)S(1)}, bf16[2048,4,64]{0,2,1:T(8,128)(2,1)}, u32[]{:S(2)}) copy-start(bf16[2048,4,64]{0,2,1:T(8,128)(2,1)} %get-tuple-element.136) | copy-start | bytes 3145732 | tf_op jit(solution)/shard_map/while
  136.7 4.4 %copy-start.9 = (s32[8]{0:T(128)S(1)}, s32[8]{0:T(128)}, u32[]{:S(2)}) copy-start(s32[8]{0:T(128)} %param.16) | copy-start | bytes 100
  136.7 9.2 %copy-start.10 = (s32[8]{0:T(128)S(1)}, s32[8]{0:T(128)}, u32[]{:S(2)}) copy-start(s32[8]{0:T(128)} %param.15) | copy-start | bytes 100
  136.7 19.4 %all-to-all-start.1 = ((bf16[4,512,256]{1,2,0:T(8,128)(2,1)}), bf16[4,512,256]{1,2,0:T(8,128)(2,1)}, u32[]{:S(2)}, u32[]{:S(2)}) async-start(bf16[4,512,256]{1,2,0:T(8,128)(2,1)} %bitcast.84), calls=%async_computation.1 | async-start | bytes 2097152 | tf_op jit(solution)/shard_map/all_to_all | solution.py:67
  146.6 9.5 %copy-start.1 = (bf16[1,512,1024]{2,1,0:T(8,128)(2,1)S(1)}, bf16[1,512,1024]{2,1,0:T(8,128)(2,1)}, u32[]{:S(2)}) copy-start(bf16[1,512,1024]{2,1,0:T(8,128)(2,1)} %param.13) | copy-start | bytes 3145732
  150.5 10.7 %collective-permute-start = (bf16[128,2048]{1,0:T(8,128)(2,1)}, bf16[128,2048]{1,0:T(8,128)(2,1)}, u32[]{:S(2)}, u32[]{:S(2)}) collective-permute-start(bf16[128,2048]{1,0:T(8,128)(2,1)} %convolution_convert_fusion.1), channel_id=1, source_target_pairs={{0,1},{1,2},{2,3},{3,0},{4,5},{5,6},{6,7},{7,4},{8,9},{9,10},{10,1... | collective-permute-start | bytes 1572872 | tf_op jit(solution)/shard_map/ppermute | solution.py:87
  156.0 5.2 %copy-start.6 = (bf16[1024,1024]{1,0:T(8,128)(2,1)S(1)}, bf16[1024,1024]{1,0:T(8,128)(2,1)}, u32[]{:S(2)}) copy-start(bf16[1024,1024]{1,0:T(8,128)(2,1)} %param.21) | copy-start | bytes 6291460
  156.0 5.2 %copy-start.8 = (f32[1024]{0:T(1024)S(1)}, f32[1024]{0:T(1024)}, u32[]{:S(2)}) copy-start(f32[1024]{0:T(1024)} %param.20) | copy-start | bytes 12292
  158.8 2.4 %copy-start.2 = (f32[512,1024]{1,0:T(8,128)}, f32[512,1024]{1,0:T(8,128)S(1)}, u32[]{:S(2)}) copy-start(f32[512,1024]{1,0:T(8,128)S(1)} %get-tuple-element.82) | copy-start | bytes 6291460
  158.8 10.5 %collective-permute-start.2 = (bf16[128,2048]{1,0:T(8,128)(2,1)}, bf16[128,2048]{1,0:T(8,128)(2,1)}, u32[]{:S(2)}, u32[]{:S(2)}) collective-permute-start(bf16[128,2048]{1,0:T(8,128)(2,1)} %convolution_convert_fusion.1), channel_id=1, source_target_pairs={{1,0},{2,1},{3,2},{0,3},{5,4},{6,5},{7,6},{4,7},{9,8},{10,9},{11,1... | collective-permute-start | bytes 1572872 | tf_op jit(solution)/shard_map/ppermute | solution.py:90
  161.2 11.5 %collective-permute-start.1 = (bf16[128,2048]{1,0:T(8,128)(2,1)}, bf16[128,2048]{1,0:T(8,128)(2,1)}, u32[]{:S(2)}, u32[]{:S(2)}) collective-permute-start(bf16[128,2048]{1,0:T(8,128)(2,1)} %collective-permute-done), channel_id=1, source_target_pairs={{0,1},{1,2},{2,3},{3,0},{4,5},{5,6},{6,7},{7,4},{8,9},{9,10},{10,1... | collective-permute-start | bytes 1572872 | tf_op jit(solution)/shard_map/ppermute | solution.py:87
  187.8 5.5 %copy-start.4 = (bf16[512,2,16,64]{0,3,2,1:T(8,128)(2,1)S(1)}, bf16[512,2,16,64]{0,3,2,1:T(8,128)(2,1)}, u32[]{:S(2)}) copy-start(bf16[512,2,16,64]{0,3,2,1:T(8,128)(2,1)} %reshape_reshape.4) | copy-start | bytes 6291460
  193.3 3.8 %copy-start.3 = (f32[512,1024]{1,0:T(8,128)S(1)}, f32[512,1024]{1,0:T(8,128)}, u32[]{:S(2)}) copy-start(f32[512,1024]{1,0:T(8,128)} %copy-done.2) | copy-start | bytes 6291460
  193.4 3.8 %copy-start.7 = (bf16[1024,1024]{1,0:T(8,128)(2,1)S(1)}, bf16[1024,1024]{1,0:T(8,128)(2,1)}, u32[]{:S(2)}) copy-start(bf16[1024,1024]{1,0:T(8,128)(2,1)} %param.23) | copy-start | bytes 6291460
Sparse Core Ops, SparseCore 0:
  35.5 52.4 all-gather.1
